TPU v7x, 32 devices: a whole 2x2x4 slice. The times are simulated.
32 devices in a mesh: dp: 2 (over core), ctx: 4 (over z), tensor: 4 (over y, x).
Axes of the slice: x: 2, y: 2, z: 4, core: 2. Of those that a mesh axis runs over, the one named last changes fastest.
Arguments:
- tokens: bfloat16 [4096, 2048], P(('dp', 'ctx')), may hold values from -6 to 6
- lengths: int32 [2, 13], P('dp'), may hold values from 1 to 819, 2048 in all within a row
- parents: int32 [2, 13], P('dp'), may hold values from 0 to 4, as said below
- w_query: bfloat16 [2048, 2048], P(('dp', 'ctx'), 'tensor'), may hold values from -0.125 to 0.125
- w_key: bfloat16 [2048, 1024], P(('dp', 'ctx'), 'tensor'), may hold values from -0.125 to 0.125
- w_value: bfloat16 [2048, 1024], P(('dp', 'ctx'), 'tensor'), may hold values from -0.125 to 0.125
- w_out: bfloat16 [2048, 2048], P('tensor', ('dp', 'ctx')), may hold values from -1.5 to 1.5
- w_gate: bfloat16 [2048, 6144], P(('dp', 'ctx'), 'tensor'), may hold values from -0.125 to 0.125
- w_up: bfloat16 [2048, 6144], P(('dp', 'ctx'), 'tensor'), may hold values from -0.125 to 0.125
- w_down: bfloat16 [6144, 2048], P('tensor', ('dp', 'ctx')), may hold values from -0.078125 to 0.078125
- gain_attn: bfloat16 [2048], P(('dp', 'ctx')), may hold values from 0.099609375 to 1.8984375
- gain_mlp: bfloat16 [2048], P(('dp', 'ctx')), may hold values from 0.099609375 to 1.8984375
- gain_query: bfloat16 [128], P(('dp', 'ctx')), may hold values from 0.099609375 to 1.8984375
- gain_key: bfloat16 [128], P(('dp', 'ctx')), may hold values from 0.099609375 to 1.8984375
- cotangent: bfloat16 [4096, 2048], P(('dp', 'ctx')), may hold values from -6 to 6
Outputs:
- result: bfloat16 [4096, 2048], P(('dp', 'ctx'))
- grad_tokens: float32 [4096, 2048], P(('dp', 'ctx'))
- grad_query: float32 [2048, 2048], P(('dp', 'ctx'), 'tensor')
- grad_key: float32 [2048, 1024], P(('dp', 'ctx'), 'tensor')
- grad_value: float32 [2048, 1024], P(('dp', 'ctx'), 'tensor')
- grad_out: float32 [2048, 2048], P('tensor', ('dp', 'ctx'))
- grad_gate: float32 [2048, 6144], P(('dp', 'ctx'), 'tensor')
- grad_up: float32 [2048, 6144], P(('dp', 'ctx'), 'tensor')
- grad_down: float32 [6144, 2048], P('tensor', ('dp', 'ctx'))
- grad_gain_attn: float32 [2048], P(('dp', 'ctx'))
- grad_gain_mlp: float32 [2048], P(('dp', 'ctx'))
- grad_gain_query: float32 [128], P(('dp', 'ctx'))
- grad_gain_key: float32 [128], P(('dp', 'ctx'))
Inputs may be any that keep to these rules, and one draw needn't show every extreme that they name: lengths[t, s] counts the tokens of segment s of tree t; the segments lie in order and each tree's lengths sum to 2048. parents[t, s] is the segment from which segment s of tree t hangs; segments 0 to 4 name 0 (segment 0 is the root), segments 5 to 12 name one of 1 to 4.
All inputs are finite; a program needn't handle non-finite values.
Results may differ from a plain program's by a relative error of at most 0.02.
Values may be sent and summed in bfloat16 or wider, within the bound.
No kernel may reach another device: no remote copies, remote signals or barrier semaphores. Data moves between devices by JAX's collectives and lax.ppermute only.
A program may use at most 192 MiB of HBM per device.

v0:
```python
import math
import jax
import jax.numpy as jnp
from jax import lax
from jax.sharding import PartitionSpec as P

HEAD_DIM = 128
EPS = 1e-06
THETA = 1000000.0
PRECISE = lax.Precision.HIGHEST
BF = jnp.bfloat16
F32 = jnp.float32
ROWS = ("dp", "ctx")


def row_scales(values):
    return lax.rsqrt(jnp.mean(values * values, axis=-1, keepdims=True) + EPS)


def norm_back(grad_in, values, gain_vec, scales):
    upstream = grad_in * gain_vec
    inner_mean = jnp.mean(upstream * values, axis=-1, keepdims=True)
    return (
        scales * upstream - values * scales * scales * scales * inner_mean,
        grad_in * values * scales,
    )


def rotate_pairs(values, cosine, sine_vals):
    half_dim = values.shape[-1] // 2
    first_half = values[..., :half_dim]
    second_half = values[..., half_dim:]
    return jnp.concatenate(
        [
            first_half * cosine - second_half * sine_vals,
            second_half * cosine + first_half * sine_vals,
        ],
        axis=-1,
    )


def rotate_back(values, cosine, sine_vals):
    return rotate_pairs(values, cosine, -sine_vals)


def dot(left, right):
    return jnp.dot(left, right, preferred_element_type=F32)


def inner_rows(left, right):
    return lax.dot_general(left, right, (((0,), (0,)), ((), ())), preferred_element_type=F32)


def outer_cols(left, right):
    return lax.dot_general(left, right, (((1,), (1,)), ((), ())), preferred_element_type=F32)


def swap(values, axis, mask):
    size = lax.axis_size(axis)
    return lax.ppermute(values, axis, [(a, a ^ mask) for a in range(size)])


def scatter_sum(partial):
    size = lax.axis_size("tensor")
    chunk = partial.shape[0] // size
    low = partial.astype(BF)
    total = partial[:chunk]
    for mask in range(1, size):
        total = total + swap(low[mask * chunk : (mask + 1) * chunk], "tensor", mask).astype(F32)
    return total


def gather_rows(own):
    size = lax.axis_size("tensor")
    return [own] + [swap(own, "tensor", mask) for mask in range(1, size)]


def xor_order(values):
    size = lax.axis_size("tensor")
    me = lax.axis_index("tensor")
    chunk = values.shape[0] // size
    return jnp.concatenate(
        [
            lax.dynamic_slice_in_dim(values, (me ^ mask) * chunk, chunk, axis=0)
            for mask in range(size)
        ],
        axis=0,
    )


def grad_scatter(left, right):
    half = left.shape[1] // 2
    me = lax.axis_index("dp")
    theirs = lax.dynamic_slice_in_dim(left, (1 - me) * half, half, axis=1)
    mine = lax.dynamic_slice_in_dim(left, me * half, half, axis=1)
    sent = swap(inner_rows(theirs, right).astype(BF), "dp", 1)
    both = (inner_rows(mine, right) + sent.astype(F32)).astype(BF)
    return lax.psum_scatter(both, "ctx", scatter_dimension=0, tiled=True)


def tree_layout(lengths, parents, tree_total):
    seg_count = lengths.shape[0]
    index = jnp.arange(seg_count, dtype=jnp.int32)
    direct = ((parents[:, None] == index[None, :]) & (parents[:, None] != index[:, None])).astype(
        F32
    )
    reach = direct
    for closure_step in range(4):
        reach = jnp.minimum(reach + jnp.dot(reach, reach, precision=PRECISE), 1.0)
    ends = jnp.cumsum(lengths, dtype=jnp.int32)
    starts = ends - lengths
    offset = jnp.dot(reach, lengths.astype(F32), precision=PRECISE)
    return (starts, reach, offset)


def segment_onehot(places, starts):
    index = jnp.arange(starts.shape[0], dtype=jnp.int32)
    member = (starts[None, :] <= places[:, None]).astype(jnp.int32)
    segment_ids = jnp.sum(member, axis=1, dtype=jnp.int32) - 1
    return (segment_ids, (segment_ids[:, None] == index[None, :]).astype(F32))


def on_device(
    tokens,
    lengths,
    parents,
    w_query,
    w_key,
    w_value,
    w_out,
    w_gate,
    w_up,
    w_down,
    gain_attn,
    gain_mlp,
    gain_query,
    gain_key,
    cotangent,
):
    row_count, width = tokens.shape
    ctx_size = lax.axis_size("ctx")
    split = lax.axis_size("tensor")
    me_t = lax.axis_index("tensor")
    chunk = row_count // split
    tree_total = row_count * ctx_size
    q_cols, k_cols = (w_query.shape[1], w_key.shape[1])
    w_qkv = lax.all_gather(
        jnp.concatenate([w_query, w_key, w_value], axis=1), ROWS, axis=0, tiled=True
    )
    wo_t = lax.all_gather(w_out.T, ROWS, axis=0, tiled=True)
    wg_full = lax.all_gather(w_gate, ROWS, axis=0, tiled=True)
    wu_full = lax.all_gather(w_up, ROWS, axis=0, tiled=True)
    wd_t = lax.all_gather(w_down.T, ROWS, axis=0, tiled=True)
    gain_sizes = (gain_attn.shape[0], gain_mlp.shape[0], gain_query.shape[0], gain_key.shape[0])
    gains = lax.all_gather(
        jnp.concatenate([gain_attn, gain_mlp, gain_query, gain_key])[None], ROWS, axis=0, tiled=True
    ).astype(F32)
    gain_parts, place = ([], 0)
    for size in gain_sizes:
        gain_parts.append(gains[:, place : place + size].reshape(-1))
        place += size
    gain_one, gain_two, gain_q, gain_k = gain_parts
    local = jnp.arange(row_count, dtype=jnp.int32)
    natural = (local // chunk ^ me_t) * chunk + local % chunk
    place_here = lax.axis_index("ctx") * row_count + natural
    place_all = (
        jnp.arange(ctx_size, dtype=jnp.int32)[:, None] * row_count + natural[None, :]
    ).reshape(-1)
    starts, reach, offset = tree_layout(lengths[0], parents[0], tree_total)
    segment_here, onehot_here = segment_onehot(place_here, starts)
    segment_all, onehot_all = segment_onehot(place_all, starts)
    position = place_here.astype(F32) + jnp.dot(
        onehot_here, offset - starts.astype(F32), precision=PRECISE
    )
    ancestor = (
        jnp.dot(jnp.dot(onehot_here, reach, precision=PRECISE), onehot_all.T, precision=PRECISE)
        > 0.5
    )
    allowed = (segment_here[:, None] == segment_all[None, :]) & (
        place_all[None, :] <= place_here[:, None]
    ) | ancestor
    half_dim = HEAD_DIM // 2
    frequency = jnp.exp(jnp.arange(half_dim, dtype=F32) * (-2.0 * math.log(THETA) / HEAD_DIM))
    angles = position[:, None] * frequency[None, :]
    cosine = jnp.cos(angles)[:, None, :]
    sine_vals = jnp.sin(angles)[:, None, :]
    score_scale = 1.0 / math.sqrt(HEAD_DIM)
    x_low = xor_order(tokens)
    g_low = xor_order(cotangent)
    inputs = x_low.astype(F32)
    scale_one = row_scales(inputs)
    normed_attn = (inputs * scale_one * gain_one).astype(BF)
    qkv = dot(normed_attn, w_qkv)
    heads_here = q_cols // HEAD_DIM
    kv_here = k_cols // HEAD_DIM
    group_size = heads_here // kv_here
    q_heads = qkv[:, :q_cols].reshape(row_count, heads_here, HEAD_DIM)
    k_heads = qkv[:, q_cols : q_cols + k_cols].reshape(row_count, kv_here, HEAD_DIM)
    v_bf = qkv[:, q_cols + k_cols :].astype(BF)
    q_scales, k_scales = (row_scales(q_heads), row_scales(k_heads))
    q_bf = rotate_pairs(q_heads * q_scales * gain_q, cosine, sine_vals).astype(BF)
    k_bf = rotate_pairs(k_heads * k_scales * gain_k, cosine, sine_vals).astype(BF)
    kv_all = lax.all_gather(
        jnp.concatenate([k_bf.reshape(row_count, k_cols), v_bf], axis=1), "ctx", axis=0, tiled=True
    )
    k_all = kv_all[:, :k_cols].reshape(tree_total, kv_here, HEAD_DIM)
    v_all = kv_all[:, k_cols:].reshape(tree_total, kv_here, HEAD_DIM)
    q_grouped = q_bf.reshape(row_count, kv_here, group_size, HEAD_DIM)
    scores = (
        jnp.einsum("tkgd,skd->kgts", q_grouped, k_all, preferred_element_type=F32) * score_scale
    )
    scores = jnp.where(allowed[None, None], scores, -1e30)
    row_max = jnp.max(scores, axis=-1, keepdims=True)
    weights = jnp.exp(scores - row_max)
    prob_all = weights / jnp.sum(weights, axis=-1, keepdims=True)
    prob_bf = prob_all.astype(BF)
    mixture = jnp.einsum("kgts,skd->tkgd", prob_bf, v_all, preferred_element_type=F32)
    mixture_bf = mixture.reshape(row_count, heads_here * HEAD_DIM).astype(BF)
    own_inputs = inputs[:chunk]
    hidden = own_inputs + scatter_sum(outer_cols(mixture_bf, wo_t))
    scale_two = row_scales(hidden)
    normed_own = (hidden * scale_two * gain_two).astype(BF)
    normed_mlp = jnp.concatenate(gather_rows(normed_own), axis=0)
    gate_pre = dot(normed_mlp, wg_full)
    up_pre = dot(normed_mlp, wu_full)
    gate_sig = jax.nn.sigmoid(gate_pre)
    gate_act = gate_pre * gate_sig
    inner_bf = (gate_act * up_pre).astype(BF)
    grad_down_t = grad_scatter(g_low, inner_bf)
    grad_inner = dot(g_low, wd_t)
    grad_gate_pre = (grad_inner * up_pre * gate_sig * (1.0 + gate_pre * (1.0 - gate_sig))).astype(
        BF
    )
    grad_up_pre = (grad_inner * gate_act).astype(BF)
    grad_normed_mlp = scatter_sum(
        outer_cols(grad_gate_pre, wg_full) + outer_cols(grad_up_pre, wu_full)
    )
    grad_gate = grad_scatter(normed_mlp, grad_gate_pre)
    grad_up = grad_scatter(normed_mlp, grad_up_pre)
    own_cotangent = g_low[:chunk].astype(F32)
    grad_hidden_norm, gain_two_terms = norm_back(grad_normed_mlp, hidden, gain_two, scale_two)
    gain_two_part = jnp.sum(gain_two_terms, axis=0)
    grad_hidden = own_cotangent + grad_hidden_norm
    grad_attn_bf = jnp.concatenate(gather_rows(grad_hidden.astype(BF)), axis=0)
    result_own = (hidden + scatter_sum(outer_cols(inner_bf, wd_t))).astype(BF)
    result = xor_order(jnp.concatenate(gather_rows(result_own), axis=0))
    grad_out_t = grad_scatter(grad_attn_bf, mixture_bf)
    grad_mixture = (
        dot(grad_attn_bf, wo_t).astype(BF).reshape(row_count, kv_here, group_size, HEAD_DIM)
    )
    grad_probs = jnp.einsum("tkgd,skd->kgts", grad_mixture, v_all, preferred_element_type=F32)
    grad_v_all = jnp.einsum("kgts,tkgd->skd", prob_bf, grad_mixture, preferred_element_type=F32)
    row_total = jnp.sum(prob_all * grad_probs, axis=-1, keepdims=True)
    grad_scores = (prob_all * (grad_probs - row_total)).astype(BF)
    grad_q = (
        jnp.einsum("kgts,skd->tkgd", grad_scores, k_all, preferred_element_type=F32) * score_scale
    )
    grad_k_all = (
        jnp.einsum("kgts,tkgd->skd", grad_scores, q_grouped, preferred_element_type=F32)
        * score_scale
    )
    grad_kv = lax.psum_scatter(
        jnp.concatenate(
            [grad_k_all.reshape(tree_total, k_cols), grad_v_all.reshape(tree_total, k_cols)], axis=1
        ).astype(BF),
        "ctx",
        scatter_dimension=0,
        tiled=True,
    )
    grad_q = grad_q.reshape(row_count, heads_here, HEAD_DIM)
    grad_k = grad_kv[:, :k_cols].reshape(row_count, kv_here, HEAD_DIM).astype(F32)
    grad_v_bf = grad_kv[:, k_cols:]
    grad_q_heads, q_gain_terms = norm_back(
        rotate_back(grad_q, cosine, sine_vals), q_heads, gain_q, q_scales
    )
    grad_k_heads, k_gain_terms = norm_back(
        rotate_back(grad_k, cosine, sine_vals), k_heads, gain_k, k_scales
    )
    grad_qkv_raw = jnp.concatenate(
        [
            grad_q_heads.reshape(row_count, q_cols).astype(BF),
            grad_k_heads.reshape(row_count, k_cols).astype(BF),
            grad_v_bf,
        ],
        axis=1,
    )
    grad_qkv = grad_scatter(normed_attn, grad_qkv_raw)
    partial_back = outer_cols(grad_qkv_raw, w_qkv)
    gain_one_part = jnp.sum(partial_back * inputs * scale_one, axis=0)
    grad_normed_attn = scatter_sum(partial_back)
    grad_input_norm, unused_terms = norm_back(
        grad_normed_attn, own_inputs, gain_one, scale_one[:chunk]
    )
    grad_own = lax.optimization_barrier((grad_hidden + grad_input_norm).astype(BF))
    grad_tokens = xor_order(jnp.concatenate(gather_rows(grad_own), axis=0)).astype(F32)
    block = lax.axis_index("dp") * ctx_size + lax.axis_index("ctx")
    summed = lax.psum(
        jnp.concatenate(
            [
                gain_one_part,
                gain_two_part,
                jnp.sum(q_gain_terms, axis=(0, 1)),
                jnp.sum(k_gain_terms, axis=(0, 1)),
            ]
        ),
        ("dp", "ctx", "tensor"),
    )
    gain_grads, place = ([], 0)
    for size, part in zip(gain_sizes, gain_parts):
        gain_grads.append(lax.dynamic_slice_in_dim(summed, place + block * size, size))
        place += part.shape[0]
    return (
        result,
        grad_tokens,
        grad_qkv[:, :q_cols].astype(F32),
        grad_qkv[:, q_cols : q_cols + k_cols].astype(F32),
        grad_qkv[:, q_cols + k_cols :].astype(F32),
        grad_out_t.T.astype(F32),
        grad_gate.astype(F32),
        grad_up.astype(F32),
        grad_down_t.T.astype(F32),
        *gain_grads,
    )


def solution(mesh):
    rows = P(ROWS, None)
    cols = P(ROWS, "tensor")
    flipped = P("tensor", ROWS)
    vector = P(ROWS)
    return jax.shard_map(
        on_device,
        mesh=mesh,
        in_specs=(
            rows,
            P("dp", None),
            P("dp", None),
            cols,
            cols,
            cols,
            flipped,
            cols,
            cols,
            flipped,
            vector,
            vector,
            vector,
            vector,
            rows,
        ),
        out_specs=(
            rows,
            rows,
            cols,
            cols,
            cols,
            flipped,
            cols,
            cols,
            flipped,
            vector,
            vector,
            vector,
            vector,
        ),
        check_vma=False,
    )
```

profile of v0, /device:TPU:0, one launch (start us, length us, event | category | flops | bytes accessed | tf_op | source)
XLA Modules:
  0.0 778.3 jit_solution(5190589777838731769)
XLA Ops:
  13.0 33.2 %all-reduce = bf16[4352]{0:T(1024)(128)(2,1)S(1)} all-reduce(bf16[4352]{0:T(1024)(128)(2,1)S(1)} %dynamic-update-slice), channel_id=2, replica_groups=mesh['dp'=2,'ctx'=4,'tensor'=4] {'dp','ctx'}, use_global_device_ids=true, to_apply=%add | all-reduce | flops 4352 | bytes 17408
  90.7 27.2 %all-gather.10.cloned.1.call-done = bf16[2048,512]{1,0:T(8,128)(2,1)} async-done(((bf16[512,512]{1,0:T(8,128)(2,1)}), bf16[2048,512]{1,0:T(8,128)(2,1)}) %all-gather.10.cloned.1.call-update) | async-done | bytes 2097168 | tf_op jit(solution)/shard_map/all_gather | solution.py:203
  126.6 11.2 %fusion.127 = (f32[2,2,512]{2,1,0:T(2,128)S(1)}, f32[2,2,512,2048]{2,3,1,0:T(8,128)}) fusion(pred[512,2048]{0,1:T(8,128)(4,1)} %copy.47, bf16[2048,2,128,1]{0,2,3,1:T(8,128)(2,1)S(1)} %copy.71, bf16[512,2,2,64]{3,0,2,1:T(8,128)(2,1)} %bitcast.198, bf16[512,2,2,64]{3,0,2,1:T(8,128)(2,1)} %bitcast.196), kind=kOutput, calls=%fused_computation.254 | convolution fusion | flops 1091569664 | bytes 19406848 | tf_op jit(solution)/shard_map/sub | solution.py:214
  157.5 9.4 %collective-permute-done = bf16[128,2048]{1,0:T(8,128)(2,1)S(1)} collective-permute-done((bf16[128,2048]{1,0:T(8,128)(2,1)S(1)}, bf16[128,2048]{1,0:T(8,128)(2,1)S(1)}, u32[]{:S(2)}, u32[]{:S(2)}) %collective-permute-start) | collective-permute-done | bytes 524320 | tf_op jit(solution)/shard_map/ppermute | solution.py:60
  166.8 11.5 %collective-permute-done.2 = bf16[128,2048]{1,0:T(8,128)(2,1)S(1)} collective-permute-done((bf16[128,2048]{1,0:T(8,128)(2,1)S(1)}, bf16[128,2048]{1,0:T(8,128)(2,1)S(1)}, u32[]{:S(2)}, u32[]{:S(2)}) %collective-permute-start.2) | collective-permute-done | bytes 524320 | tf_op jit(solution)/shard_map/ppermute | solution.py:60
  183.9 30.7 %all-gather.18.cloned.1.call-done = bf16[2048,1536]{0,1:T(8,128)(2,1)} async-done(((bf16[256,1536]{0,1:T(8,128)(2,1)}), bf16[2048,1536]{0,1:T(8,128)(2,1)}) %all-gather.18.cloned.1.call-update) | async-done | bytes 6291472 | tf_op jit(solution)/shard_map/all_gather | solution.py:153
  222.7 56.2 %all-gather.16.cloned.1.call-done = bf16[2048,1536]{1,0:T(8,128)(2,1)} async-done(((bf16[256,1536]{1,0:T(8,128)(2,1)}), bf16[2048,1536]{1,0:T(8,128)(2,1)}) %all-gather.16.cloned.1.call-update) | async-done | bytes 6291472 | tf_op jit(solution)/shard_map/all_gather | solution.py:152
  279.0 8.5 %fusion.114 = f32[512,1536]{1,0:T(8,128)} fusion(bf16[2048,1536]{1,0:T(8,128)(2,1)} %all-gather.16.cloned.1.call-done, bf16[128,2048]{1,0:T(8,128)(2,1)} %collective-permute-done.5, bf16[128,2048]{1,0:T(8,128)(2,1)} %collective-permute-done.4, bf16[128,2048]{1,0:T(8,128)(2,1)} %collective-permute-done.3, bf16[128,2048]{1,0:T(8,128)(2,1)S(1)} %multiply_convert_fusion.4), kind=kOutput, calls=%fused_computation.243 | convolution fusion | flops 3229614080 | bytes 11534336 | tf_op jit(solution)/shard_map/dot_general | solution.py:47
  287.4 56.3 %all-gather.14.cloned.1.call-done = bf16[2048,1536]{1,0:T(8,128)(2,1)} async-done(((bf16[256,1536]{1,0:T(8,128)(2,1)}), bf16[2048,1536]{1,0:T(8,128)(2,1)}) %all-gather.14.cloned.1.call-update) | async-done | bytes 6291472 | tf_op jit(solution)/shard_map/all_gather | solution.py:151
  343.8 11.2 %multiply_convert_fusion.1 = (bf16[512,1536]{1,0:T(8,128)(2,1)S(1)}, bf16[512,1536]{1,0:T(8,128)(2,1)S(1)}, bf16[512,1536]{1,0:T(8,128)(2,1)}) fusion(f32[512,1536]{1,0:T(8,128)} %fusion.112, f32[512,1536]{1,0:T(8,128)} %fusion.114, bf16[2048,1536]{1,0:T(8,128)(2,1)} %all-gather.14.cloned.1.call-done, bf16[128,2048]{1,0:T(8,128)(2,1)} %collective-permute-done.5, ...), kind=kOutput, calls=%fused_computation.28 | convolution fusion | flops 3241410560 | bytes 19398656 | tf_op jit(solution)/shard_map/dot_general | solution.py:47
  369.0 11.3 %collective-permute-done.12 = bf16[128,2048]{1,0:T(8,128)(2,1)S(1)} collective-permute-done((bf16[128,2048]{1,0:T(8,128)(2,1)S(1)}, bf16[128,2048]{1,0:T(8,128)(2,1)S(1)}, u32[]{:S(2)}, u32[]{:S(2)}) %collective-permute-start.12) | collective-permute-done | bytes 524320 | tf_op jit(solution)/shard_map/ppermute | solution.py:60
  380.4 11.5 %collective-permute-done.14 = bf16[128,2048]{1,0:T(8,128)(2,1)S(1)} collective-permute-done((bf16[128,2048]{1,0:T(8,128)(2,1)S(1)}, bf16[128,2048]{1,0:T(8,128)(2,1)S(1)}, u32[]{:S(2)}, u32[]{:S(2)}) %collective-permute-start.14) | collective-permute-done | bytes 524320 | tf_op jit(solution)/shard_map/ppermute | solution.py:60
  397.8 12.2 %collective-permute-done.17 = bf16[128,2048]{1,0:T(8,128)(2,1)S(1)} collective-permute-done((bf16[128,2048]{1,0:T(8,128)(2,1)S(1)}, bf16[128,2048]{1,0:T(8,128)(2,1)S(1)}, u32[]{:S(2)}, u32[]{:S(2)}) %collective-permute-start.17) | collective-permute-done | bytes 524320 | tf_op jit(solution)/shard_map/ppermute | solution.py:60
  410.0 9.1 %collective-permute-done.16 = bf16[128,2048]{1,0:T(8,128)(2,1)S(1)} collective-permute-done((bf16[128,2048]{1,0:T(8,128)(2,1)S(1)}, bf16[128,2048]{1,0:T(8,128)(2,1)S(1)}, u32[]{:S(2)}, u32[]{:S(2)}) %collective-permute-start.16) | collective-permute-done | bytes 524320 | tf_op jit(solution)/shard_map/ppermute | solution.py:60
  420.4 9.7 %fusion.18 = bf16[2,128,2048]{2,1,0:T(8,128)(2,1)} fusion(bf16[512,2,2,128]{0,3,2,1:T(8,128)(2,1)S(1)} %bitcast.227, f32[2,2,512,2048]{2,3,1,0:T(8,128)} %get-tuple-element.115, f32[2,2,512]{2,1,0:T(2,128)S(1)} %get-tuple-element.114), kind=kOutput, calls=%fused_computation.38 | convolution fusion | flops 1082654720 | bytes 18358272 | tf_op jit(solution)/shard_map/kgts,tkgd->skd/dot_general | solution.py:252
  430.2 10.7 %fusion.1 = (f32[2,2,512]{2,1,0:T(2,128)S(1)}, f32[2,2048,512,2]{2,1,3,0:T(8,128)}) fusion(f32[2,2,512,2048]{2,3,1,0:T(8,128)} %get-tuple-element.115, f32[2,2,512]{2,1,0:T(2,128)S(1)} %get-tuple-element.114, bf16[512,2,2,128]{0,3,2,1:T(8,128)(2,1)S(1)} %bitcast.228, bf16[2048,2,128,1]{2,1,0,3:T(2,128)(2,1)S(1)} %bitcast.205), kind=kOutput, calls=%fused_computation.3 | convolution fusion | flops 1086322688 | bytes 35143680 | tf_op jit(solution)/shard_map/tkgd,skd->kgts/dot_general | solution.py:251
  443.1 12.1 %fusion.3 = bf16[2,2,512,2048]{2,3,1,0:T(8,128)(2,1)S(1)} fusion(f32[2,2048,512,2]{2,1,3,0:T(8,128)} %get-tuple-element.121, f32[2,2,512]{2,1,0:T(2,128)S(1)} %get-tuple-element.120, f32[2,2,512,2048]{2,3,1,0:T(8,128)} %get-tuple-element.115, f32[2,2,512]{2,1,0:T(2,128)S(1)} %get-tuple-element.114), kind=kLoop, calls=%fused_computation.5 | loop fusion | flops 16777216 | bytes 41959424 | tf_op jit(solution)/shard_map/convert_element_type | solution.py:254
  573.9 10.8 %collective-permute-done.20 = bf16[128,2048]{1,0:T(8,128)(2,1)} collective-permute-done((bf16[128,2048]{1,0:T(8,128)(2,1)}, bf16[128,2048]{1,0:T(8,128)(2,1)}, u32[]{:S(2)}, u32[]{:S(2)}) %collective-permute-start.20) | collective-permute-done | bytes 524320 | tf_op jit(solution)/shard_map/ppermute | solution.py:60
  596.0 10.4 %collective-permute-done.8 = bf16[128,2048]{1,0:T(8,128)(2,1)} collective-permute-done((bf16[128,2048]{1,0:T(8,128)(2,1)}, bf16[128,2048]{1,0:T(8,128)(2,1)}, u32[]{:S(2)}, u32[]{:S(2)}) %collective-permute-start.8) | collective-permute-done | bytes 524320 | tf_op jit(solution)/shard_map/ppermute | solution.py:60
  617.9 52.7 %psum.7 = f32[4352]{0:T(1024)S(1)} all-reduce(f32[4352]{0:T(1024)S(1)} %pad_maximum_fusion.15), channel_id=1, replica_groups=mesh['dp'=2,'ctx'=4,'tensor'=4] {'dp','ctx','tensor'}, use_global_device_ids=true, to_apply=%region_26.27 | all-reduce | flops 4352 | bytes 34816 | tf_op jit(solution)/shard_map/psum | solution.py:297
  677.1 10.7 %collective-permute-done.11 = bf16[128,2048]{1,0:T(8,128)(2,1)S(1)} collective-permute-done((bf16[128,2048]{1,0:T(8,128)(2,1)}, bf16[128,2048]{1,0:T(8,128)(2,1)S(1)}, u32[]{:S(2)}, u32[]{:S(2)}) %collective-permute-start.11) | collective-permute-done | bytes 524320 | tf_op jit(solution)/shard_map/ppermute | solution.py:60
  687.8 9.3 %collective-permute-done.10 = bf16[128,2048]{1,0:T(8,128)(2,1)S(1)} collective-permute-done((bf16[128,2048]{1,0:T(8,128)(2,1)}, bf16[128,2048]{1,0:T(8,128)(2,1)S(1)}, u32[]{:S(2)}, u32[]{:S(2)}) %collective-permute-start.10) | collective-permute-done | bytes 524320 | tf_op jit(solution)/shard_map/ppermute | solution.py:60
  707.2 14.8 %reduce-scatter.15.cloned.1.call-done = bf16[256,1536]{1,0:T(8,128)(2,1)} async-done(((bf16[1024,1536]{1,0:T(8,128)(2,1)}), bf16[256,1536]{1,0:T(8,128)(2,1)}) %reduce-scatter.15.cloned.1.call-update) | async-done | bytes 786448 | tf_op jit(solution)/shard_map/reduce_scatter | solution.py:98
  724.4 43.3 %reduce-scatter.9.cloned.1.call-done = bf16[256,1024]{1,0:T(8,128)(2,1)} async-done(((bf16[1024,1024]{1,0:T(8,128)(2,1)}), bf16[256,1024]{1,0:T(8,128)(2,1)}) %reduce-scatter.9.cloned.1.call-update) | async-done | bytes 524304 | tf_op jit(solution)/shard_map/reduce_scatter | solution.py:98
  (368 shorter events, 278.0 us)
Async XLA Ops:
  7.2 53.6 %all-gather.8.cloned.1.call-start = ((), (), s32[]{:S(2)}) async-start(), calls=%async_computation.6 | async-start | bytes 4718592 | tf_op jit(solution)/shard_map/all_gather | solution.py:147
  9.2 108.7 %all-gather.10.cloned.1.call-start = ((), (), s32[]{:S(2)}) async-start(), calls=%async_computation.7 | async-start | bytes 2621440 | tf_op jit(solution)/shard_map/all_gather | solution.py:203
  73.2 75.7 %all-gather.12.cloned.1.call-start = ((), (), s32[]{:S(2)}) async-start(), calls=%async_computation.8 | async-start | bytes 2359296 | tf_op jit(solution)/shard_map/all_gather | solution.py:150
  74.0 140.6 %all-gather.18.cloned.1.call-start = ((), (), s32[]{:S(2)}) async-start(), calls=%async_computation.11 | async-start | bytes 7077888 | tf_op jit(solution)/shard_map/all_gather | solution.py:153
  74.5 204.4 %all-gather.16.cloned.1.call-start = ((), (), s32[]{:S(2)}) async-start(), calls=%async_computation.10 | async-start | bytes 7077888 | tf_op jit(solution)/shard_map/all_gather | solution.py:152
  75.1 268.7 %all-gather.14.cloned.1.call-start = ((), (), s32[]{:S(2)}) async-start(), calls=%async_computation.9 | async-start | bytes 7077888 | tf_op jit(solution)/shard_map/all_gather | solution.py:151
  75.7 459.8 %reduce-scatter.7.cloned.1.call-start = ((), (), s32[]{:S(2)}) async-start(), calls=%async_computation.12 | async-start | bytes 2621440 | tf_op jit(solution)/shard_map/reduce_scatter | solution.py:262
  153.4 24.8 %collective-permute-start.2 = (bf16[128,2048]{1,0:T(8,128)(2,1)S(1)}, bf16[128,2048]{1,0:T(8,128)(2,1)S(1)}, u32[]{:S(2)}, u32[]{:S(2)}) collective-permute-start(bf16[128,2048]{1,0:T(8,128)(2,1)S(1)} %get-tuple-element.81), channel_id=1, source_target_pairs={{0,3},{1,2},{2,1},{3,0},{4,7},{5,6},{6,5},{7,4},{8,11},{9,10},{10,... | collective-permute-start | bytes 1572872 | tf_op jit(solution)/shard_map/ppermute | solution.py:60
  180.3 98.7 %collective-permute-start.5 = (bf16[128,2048]{1,0:T(8,128)(2,1)S(1)}, bf16[128,2048]{1,0:T(8,128)(2,1)}, u32[]{:S(2)}, u32[]{:S(2)}) collective-permute-start(bf16[128,2048]{1,0:T(8,128)(2,1)S(1)} %multiply_convert_fusion.4), channel_id=1, source_target_pairs={{0,3},{1,2},{2,1},{3,0},{4,7},{5,6},{6,5},{7,4},{8,11},{9,10},{10,... | collective-permute-start | bytes 1572872 | tf_op jit(solution)/shard_map/ppermute | solution.py:60
  181.8 97.1 %collective-permute-start.4 = (bf16[128,2048]{1,0:T(8,128)(2,1)S(1)}, bf16[128,2048]{1,0:T(8,128)(2,1)}, u32[]{:S(2)}, u32[]{:S(2)}) collective-permute-start(bf16[128,2048]{1,0:T(8,128)(2,1)S(1)} %multiply_convert_fusion.4), channel_id=1, source_target_pairs={{0,2},{1,3},{2,0},{3,1},{4,6},{5,7},{6,4},{7,5},{8,10},{9,11},{10,... | collective-permute-start | bytes 1572872 | tf_op jit(solution)/shard_map/ppermute | solution.py:60
  183.3 95.7 %collective-permute-start.3 = (bf16[128,2048]{1,0:T(8,128)(2,1)S(1)}, bf16[128,2048]{1,0:T(8,128)(2,1)}, u32[]{:S(2)}, u32[]{:S(2)}) collective-permute-start(bf16[128,2048]{1,0:T(8,128)(2,1)S(1)} %multiply_convert_fusion.4), channel_id=1, source_target_pairs={{0,1},{1,0},{2,3},{3,2},{4,5},{5,4},{6,7},{7,6},{8,9},{9,8},{10,11... | collective-permute-start | bytes 1572872 | tf_op jit(solution)/shard_map/ppermute | solution.py:60
  464.3 151.6 %reduce-scatter.11.cloned.1.call-start = ((), (), s32[]{:S(2)}) async-start(), calls=%async_computation.14 | async-start | bytes 1310720 | tf_op jit(solution)/shard_map/reduce_scatter | solution.py:98
  480.6 221.2 %reduce-scatter.17.cloned.1.call-start = ((), (), s32[]{:S(2)}) async-start(), calls=%async_computation.17 | async-start | bytes 3932160 | tf_op jit(solution)/shard_map/reduce_scatter | solution.py:98
  486.9 217.8 %reduce-scatter.13.cloned.1.call-start = ((), (), s32[]{:S(2)}) async-start(), calls=%async_computation.15 | async-start | bytes 3932160 | tf_op jit(solution)/shard_map/reduce_scatter | solution.py:98
  500.9 221.0 %reduce-scatter.15.cloned.1.call-start = ((), (), s32[]{:S(2)}) async-start(), calls=%async_computation.16 | async-start | bytes 3932160 | tf_op jit(solution)/shard_map/reduce_scatter | solution.py:98
  518.8 248.9 %reduce-scatter.9.cloned.1.call-start = ((), (), s32[]{:S(2)}) async-start(), calls=%async_computation.13 | async-start | bytes 2621440 | tf_op jit(solution)/shard_map/reduce_scatter | solution.py:98
  559.1 25.5 %collective-permute-start.20 = (bf16[128,2048]{1,0:T(8,128)(2,1)}, bf16[128,2048]{1,0:T(8,128)(2,1)}, u32[]{:S(2)}, u32[]{:S(2)}) collective-permute-start(bf16[128,2048]{1,0:T(8,128)(2,1)} %get-tuple-element.64), channel_id=1, source_target_pairs={{0,3},{1,2},{2,1},{3,0},{4,7},{5,6},{6,5},{7,4},{8,11},{9,10},{10,... | collective-permute-start | bytes 1572872 | tf_op jit(solution)/shard_map/ppermute | solution.py:60
  560.3 26.3 %collective-permute-start.19 = (bf16[128,2048]{1,0:T(8,128)(2,1)}, bf16[128,2048]{1,0:T(8,128)(2,1)}, u32[]{:S(2)}, u32[]{:S(2)}) collective-permute-start(bf16[128,2048]{1,0:T(8,128)(2,1)} %get-tuple-element.65), channel_id=1, source_target_pairs={{0,2},{1,3},{2,0},{3,1},{4,6},{5,7},{6,4},{7,5},{8,10},{9,11},{10,... | collective-permute-start | bytes 1572872 | tf_op jit(solution)/shard_map/ppermute | solution.py:60
  563.0 33.0 %collective-permute-start.6 = (bf16[128,2048]{1,0:T(8,128)(2,1)}, bf16[128,2048]{1,0:T(8,128)(2,1)}, u32[]{:S(2)}, u32[]{:S(2)}) collective-permute-start(bf16[128,2048]{1,0:T(8,128)(2,1)} %get-tuple-element.77), channel_id=1, source_target_pairs={{0,1},{1,0},{2,3},{3,2},{4,5},{5,4},{6,7},{7,6},{8,9},{9,8},{10,11... | collective-permute-start | bytes 1572872 | tf_op jit(solution)/shard_map/ppermute | solution.py:60
  563.8 42.6 %collective-permute-start.8 = (bf16[128,2048]{1,0:T(8,128)(2,1)}, bf16[128,2048]{1,0:T(8,128)(2,1)}, u32[]{:S(2)}, u32[]{:S(2)}) collective-permute-start(bf16[128,2048]{1,0:T(8,128)(2,1)} %get-tuple-element.78), channel_id=1, source_target_pairs={{0,3},{1,2},{2,1},{3,0},{4,7},{5,6},{6,5},{7,4},{8,11},{9,10},{10,... | collective-permute-start | bytes 1572872 | tf_op jit(solution)/shard_map/ppermute | solution.py:60
  573.4 34.3 %collective-permute-start.7 = (bf16[128,2048]{1,0:T(8,128)(2,1)}, bf16[128,2048]{1,0:T(8,128)(2,1)S(1)}, u32[]{:S(2)}, u32[]{:S(2)}) collective-permute-start(bf16[128,2048]{1,0:T(8,128)(2,1)} %get-tuple-element.79), channel_id=1, source_target_pairs={{0,2},{1,3},{2,0},{3,1},{4,6},{5,7},{6,4},{7,5},{8,10},{9,11},{10,... | collective-permute-start | bytes 1572872 | tf_op jit(solution)/shard_map/ppermute | solution.py:60
  612.4 63.2 %collective-permute-start.23 = (bf16[128,2048]{1,0:T(8,128)(2,1)}, bf16[128,2048]{1,0:T(8,128)(2,1)S(1)}, u32[]{:S(2)}, u32[]{:S(2)}) collective-permute-start(bf16[128,2048]{1,0:T(8,128)(2,1)} %get-tuple-element.91), channel_id=1, source_target_pairs={{0,3},{1,2},{2,1},{3,0},{4,7},{5,6},{6,5},{7,4},{8,11},{9,10},{10,... | collective-permute-start | bytes 1572872 | tf_op jit(solution)/shard_map/ppermute | solution.py:60
  614.2 61.5 %collective-permute-start.22 = (bf16[128,2048]{1,0:T(8,128)(2,1)}, bf16[128,2048]{1,0:T(8,128)(2,1)S(1)}, u32[]{:S(2)}, u32[]{:S(2)}) collective-permute-start(bf16[128,2048]{1,0:T(8,128)(2,1)} %get-tuple-element.91), channel_id=1, source_target_pairs={{0,2},{1,3},{2,0},{3,1},{4,6},{5,7},{6,4},{7,5},{8,10},{9,11},{10,... | collective-permute-start | bytes 1572872 | tf_op jit(solution)/shard_map/ppermute | solution.py:60
  615.3 60.3 %collective-permute-start.21 = (bf16[128,2048]{1,0:T(8,128)(2,1)}, bf16[128,2048]{1,0:T(8,128)(2,1)S(1)}, u32[]{:S(2)}, u32[]{:S(2)}) collective-permute-start(bf16[128,2048]{1,0:T(8,128)(2,1)} %get-tuple-element.91), channel_id=1, source_target_pairs={{0,1},{1,0},{2,3},{3,2},{4,5},{5,4},{6,7},{7,6},{8,9},{9,8},{10,11... | collective-permute-start | bytes 1572872 | tf_op jit(solution)/shard_map/ppermute | solution.py:60
  (91 other events, 1503.8 us)
Sparse Core Ops, SparseCore 0:
  10.2 50.5 all-gather.7
  73.3 44.5 all-gather.9
  119.5 29.4 all-gather.11
  150.4 64.1 all-gather.17
  216.0 62.8 all-gather.15
  280.4 63.3 all-gather.13
  464.4 41.3 reduce-scatter.6
  508.2 26.4 reduce-scatter.10
  537.0 58.9 reduce-scatter.16
  598.1 61.0 reduce-scatter.12
  661.5 60.4 reduce-scatter.14
  724.1 43.5 reduce-scatter.8
where the time goes:
time: 786 us; the launch traced here: 778 us
  waiting for transfers between devices  376 us (48%)
  matrix products  147 us (19%)
  blocking collectives  86 us (11%)
  other arithmetic  73.9 us (9%)
  local copies, waits for them, and re-layouts  49.5 us (6%)
  starting transfers between devices  29.6 us (4%)
  between operations  16.3 us (2%)
    ppermute x29, waiting for transfers between devices, swap(): return lax.ppermute(values, axis, [(a, a ^ mask) for a in range(size)])  140 us
    reduce_scatter x5, waiting for transfers between devices, grad_scatter(): return lax.psum_scatter(both, 'ctx', scatter_dimension=0, tiled=True)  58 us
    all_gather x1, waiting for transfers between devices, on_device(): wg_full = lax.all_gather(w_gate, ROWS, axis=0, tiled=True)  56.3 us
    all_gather x1, waiting for transfers between devices, on_device(): wu_full = lax.all_gather(w_up, ROWS, axis=0, tiled=True)  56.2 us
    psum x1, blocking collectives, on_device(): lax.psum(jnp.concatenate([gain_one_part, gain_two_part, jnp.sum(q_gain_te...  52.7 us
    dot_general x10, matrix products, inner_rows(): lax.dot_general(left, right, (((0,), (0,)), ((), ())), preferred_element_...  35.8 us
    dot_general x5, matrix products, dot(): return jnp.dot(left, right, preferred_element_type=F32)  34.2 us
    unnamed x1, blocking collectives  33.2 us
  transfers between devices with their start and end apart: 41, of which 27 were waited for; matrix products, arithmetic and copies ran while one was open for 23% of the time, Pallas kernels for 0%

commit v1 on v0

--- a/solution.py
+++ b/solution.py
@@ -3,6 +3,7 @@
 import jax.numpy as jnp
 from jax import lax
 from jax.sharding import PartitionSpec as P
+from jax.lax import axis_index, axis_size, ppermute
 
 HEAD_DIM = 128
 EPS = 1e-06
@@ -11,6 +12,16 @@
 BF = jnp.bfloat16
 F32 = jnp.float32
 ROWS = ("dp", "ctx")
+
+
+def use_pipes(local_block, dimension_no):
+    local_block = jnp.moveaxis(local_block, 0, dimension_no)
+    base_arr = local_block.shape
+    return local_block.reshape(
+        *base_arr[:dimension_no],
+        base_arr[dimension_no] * base_arr[dimension_no + 1],
+        *base_arr[dimension_no + 2 :]
+    )
 
 
 def row_scales(values):
@@ -148,7 +159,31 @@
         jnp.concatenate([w_query, w_key, w_value], axis=1), ROWS, axis=0, tiled=True
     )
     wo_t = lax.all_gather(w_out.T, ROWS, axis=0, tiled=True)
-    wg_full = lax.all_gather(w_gate, ROWS, axis=0, tiled=True)
+
+    def _detail_matrix(shard_in, a_name, k_dim):
+        n_blocks = axis_size(a_name)
+        entries = []
+        for w in range(n_blocks):
+            entries.append((w, (w + 1) % n_blocks))
+        queue = []
+        for m, k0 in entries:
+            queue.append((k0, m))
+        reached, kept_arr = ([], [])
+        for s in range(n_blocks - 1):
+            if s % 2 == 0:
+                x_now = ppermute(reached[-1] if reached else shard_in, a_name, entries)
+                reached.append(x_now)
+            else:
+                arr_next = ppermute(kept_arr[-1] if kept_arr else shard_in, a_name, queue)
+                kept_arr.append(arr_next)
+        p_next = jnp.stack([*reached[::-1], shard_in, *kept_arr])
+        raw_out = axis_index(a_name)
+        moved = len(reached)
+        k_now = raw_out - moved
+        p_next = p_next[(jnp.arange(n_blocks) - k_now) % n_blocks]
+        return use_pipes(p_next, k_dim)
+
+    wg_full = _detail_matrix(w_gate, ROWS, 0)
     wu_full = lax.all_gather(w_up, ROWS, axis=0, tiled=True)
     wd_t = lax.all_gather(w_down.T, ROWS, axis=0, tiled=True)
     gain_sizes = (gain_attn.shape[0], gain_mlp.shape[0], gain_query.shape[0], gain_key.shape[0])

time: 786 us -> 812 us (1.033)
  local copies, waits for them, and re-layouts: 49.5 us -> 63.6 us
  starting transfers between devices: 29.6 us -> 42.5 us
    ppermute x0 -> x7, waiting for transfers between devices: none -> 131 us  [the longest x4 103 us: _detail_matrix(): x_now = ppermute(reached[-1] if reached else shard_in, a_name, entries)]
    all_gather x1 -> x0, waiting for transfers between devices: 56.3 us -> none  [on_device(): wg_full = lax.all_gather(w_gate, ROWS, axis=0, tiled=True)]
    all_gather x1, waiting for transfers between devices: 30.7 us -> 0.01 us  [on_device(): wd_t = lax.all_gather(w_down.T, ROWS, axis=0, tiled=True)]
    all_gather x1, waiting for transfers between devices: 27.2 us -> 0.01 us  [on_device(): lax.all_gather(jnp.concatenate([k_bf.reshape(row_count, k_cols), v_bf], a...]
    ppermute x0 -> x7, starting transfers between devices: none -> 12.2 us  [the longest x4 11.7 us: _detail_matrix(): x_now = ppermute(reached[-1] if reached else shard_in, a_name, entries)]
    ppermute x29, waiting for transfers between devices: 140 us -> 129 us  [swap(): return lax.ppermute(values, axis, [(a, a ^ mask) for a in range(size)])]
    unnamed x158 -> x183, local copies, waits for them, and re-layouts: 14.5 us -> 23.9 us
  transfers between devices with their start and end apart: 41 -> 47, of which waited for: 27 -> 29; matrix products, arithmetic and copies ran while one was open for 23% -> 24% of each run, Pallas kernels for 0% -> 0%
where the time goes in v1:
time: 812 us; the launch traced here: 803 us
  waiting for transfers between devices  375 us (46%)
  matrix products  143 us (18%)
  blocking collectives  86.4 us (11%)
  other arithmetic  76.5 us (9%)
  local copies, waits for them, and re-layouts  63.6 us (8%)
  starting transfers between devices  42.5 us (5%)
  between operations  16.2 us (2%)
    ppermute x29, waiting for transfers between devices, swap(): return lax.ppermute(values, axis, [(a, a ^ mask) for a in range(size)])  129 us
    ppermute x4, waiting for transfers between devices, _detail_matrix(): x_now = ppermute(reached[-1] if reached else shard_in, a_name, entries)  103 us
    reduce_scatter x5, waiting for transfers between devices, grad_scatter(): return lax.psum_scatter(both, 'ctx', scatter_dimension=0, tiled=True)  58 us
    all_gather x1, waiting for transfers between devices, on_device(): wu_full = lax.all_gather(w_up, ROWS, axis=0, tiled=True)  53.5 us
    psum x1, blocking collectives, on_device(): lax.psum(jnp.concatenate([gain_one_part, gain_two_part, jnp.sum(q_gain_te...  53.2 us
    dot_general x10, matrix products, inner_rows(): lax.dot_general(left, right, (((0,), (0,)), ((), ())), preferred_element_...  36 us
    unnamed x1, blocking collectives  33.2 us
    dot_general x5, matrix products, dot(): return jnp.dot(left, right, preferred_element_type=F32)  30.3 us
  transfers between devices with their start and end apart: 47, of which 29 were waited for; matrix products, arithmetic and copies ran while one was open for 24% of the time, Pallas kernels for 0%

profile of v1, /device:TPU:0, one launch (start us, length us, event | category | flops | bytes accessed | tf_op | source)
XLA Modules:
  0.0 803.2 jit_solution(10005455635735425830)
XLA Ops:
  13.0 33.2 %all-reduce = bf16[4352]{0:T(1024)(128)(2,1)S(1)} all-reduce(bf16[4352]{0:T(1024)(128)(2,1)S(1)} %dynamic-update-slice), channel_id=2, replica_groups=mesh['dp'=2,'ctx'=4,'tensor'=4] {'dp','ctx'}, use_global_device_ids=true, to_apply=%add | all-reduce | flops 4352 | bytes 17408
  74.8 33.0 %collective-permute-done.6 = bf16[256,1536]{1,0:T(8,128)(2,1)} collective-permute-done((bf16[256,1536]{1,0:T(8,128)(2,1)}, bf16[256,1536]{1,0:T(8,128)(2,1)}, u32[]{:S(2)}, u32[]{:S(2)}) %collective-permute-start.6) | collective-permute-done | bytes 786464 | tf_op jit(solution)/shard_map/ppermute | solution.py:174
  107.8 10.3 %collective-permute-start.7 = (bf16[256,1536]{1,0:T(8,128)(2,1)}, bf16[256,1536]{1,0:T(8,128)(2,1)}, u32[]{:S(2)}, u32[]{:S(2)}) collective-permute-start(bf16[256,1536]{1,0:T(8,128)(2,1)} %collective-permute-done.6), channel_id=1, source_target_pairs={{0,4},{4,8},{8,12},{12,16},{16,20},{20,24},{24,28},{28,0},{1,5},{5... | collective-permute-start | bytes 2359304 | tf_op jit(solution)/shard_map/ppermute | solution.py:174
  118.4 27.8 %collective-permute-done.7 = bf16[256,1536]{1,0:T(8,128)(2,1)} collective-permute-done((bf16[256,1536]{1,0:T(8,128)(2,1)}, bf16[256,1536]{1,0:T(8,128)(2,1)}, u32[]{:S(2)}, u32[]{:S(2)}) %collective-permute-start.7) | collective-permute-done | bytes 786464 | tf_op jit(solution)/shard_map/ppermute | solution.py:174
  155.1 12.8 %collective-permute-done.10 = bf16[256,1536]{1,0:T(8,128)(2,1)} collective-permute-done((bf16[256,1536]{1,0:T(8,128)(2,1)}, bf16[256,1536]{1,0:T(8,128)(2,1)}, u32[]{:S(2)}, u32[]{:S(2)}) %collective-permute-start.10) | collective-permute-done | bytes 786464 | tf_op jit(solution)/shard_map/ppermute | solution.py:177
  167.9 26.9 %collective-permute-done.8 = bf16[256,1536]{1,0:T(8,128)(2,1)} collective-permute-done((bf16[256,1536]{1,0:T(8,128)(2,1)}, bf16[256,1536]{1,0:T(8,128)(2,1)}, u32[]{:S(2)}, u32[]{:S(2)}) %collective-permute-start.8) | collective-permute-done | bytes 786464 | tf_op jit(solution)/shard_map/ppermute | solution.py:174
  200.2 15.3 %collective-permute-done.11 = bf16[256,1536]{1,0:T(8,128)(2,1)} collective-permute-done((bf16[256,1536]{1,0:T(8,128)(2,1)}, bf16[256,1536]{1,0:T(8,128)(2,1)}, u32[]{:S(2)}, u32[]{:S(2)}) %collective-permute-start.11) | collective-permute-done | bytes 786464 | tf_op jit(solution)/shard_map/ppermute | solution.py:177
  216.0 15.5 %collective-permute-done.9 = bf16[256,1536]{1,0:T(8,128)(2,1)S(1)} collective-permute-done((bf16[256,1536]{1,0:T(8,128)(2,1)}, bf16[256,1536]{1,0:T(8,128)(2,1)S(1)}, u32[]{:S(2)}, u32[]{:S(2)}) %collective-permute-start.9) | collective-permute-done | bytes 786464 | tf_op jit(solution)/shard_map/ppermute | solution.py:174
  248.3 11.5 %fusion.129 = (f32[2,2,512]{2,1,0:T(2,128)S(1)}, f32[2,2,512,2048]{2,3,1,0:T(8,128)}) fusion(pred[512,2048]{0,1:T(8,128)(4,1)} %copy.47, bf16[2048,2,128,1]{0,2,3,1:T(8,128)(2,1)S(1)} %copy.71, bf16[512,2,2,64]{3,0,2,1:T(8,128)(2,1)} %bitcast.221, bf16[512,2,2,64]{3,0,2,1:T(8,128)(2,1)S(1)} %bitcast.219), kind=kOutput, calls=%fused_computation.270 | convolution fusion | flops 1091569664 | bytes 19406848 | tf_op jit(solution)/shard_map/sub | solution.py:249
  287.5 9.2 %collective-permute-done.2 = bf16[128,2048]{1,0:T(8,128)(2,1)S(1)} collective-permute-done((bf16[128,2048]{1,0:T(8,128)(2,1)}, bf16[128,2048]{1,0:T(8,128)(2,1)S(1)}, u32[]{:S(2)}, u32[]{:S(2)}) %collective-permute-start.2) | collective-permute-done | bytes 524320 | tf_op jit(solution)/shard_map/ppermute | solution.py:71
  314.5 53.5 %all-gather.13.cloned.1.call-done = bf16[2048,1536]{1,0:T(8,128)(2,1)} async-done(((bf16[256,1536]{1,0:T(8,128)(2,1)}), bf16[2048,1536]{1,0:T(8,128)(2,1)}) %all-gather.13.cloned.1.call-update) | async-done | bytes 6291472 | tf_op jit(solution)/shard_map/all_gather | solution.py:187
  394.4 11.3 %collective-permute-done.19 = bf16[128,2048]{1,0:T(8,128)(2,1)S(1)} collective-permute-done((bf16[128,2048]{1,0:T(8,128)(2,1)S(1)}, bf16[128,2048]{1,0:T(8,128)(2,1)S(1)}, u32[]{:S(2)}, u32[]{:S(2)}) %collective-permute-start.19) | collective-permute-done | bytes 524320 | tf_op jit(solution)/shard_map/ppermute | solution.py:71
  405.7 11.5 %collective-permute-done.21 = bf16[128,2048]{1,0:T(8,128)(2,1)S(1)} collective-permute-done((bf16[128,2048]{1,0:T(8,128)(2,1)S(1)}, bf16[128,2048]{1,0:T(8,128)(2,1)S(1)}, u32[]{:S(2)}, u32[]{:S(2)}) %collective-permute-start.21) | collective-permute-done | bytes 524320 | tf_op jit(solution)/shard_map/ppermute | solution.py:71
  423.2 12.2 %collective-permute-done.24 = bf16[128,2048]{1,0:T(8,128)(2,1)S(1)} collective-permute-done((bf16[128,2048]{1,0:T(8,128)(2,1)S(1)}, bf16[128,2048]{1,0:T(8,128)(2,1)S(1)}, u32[]{:S(2)}, u32[]{:S(2)}) %collective-permute-start.24) | collective-permute-done | bytes 524320 | tf_op jit(solution)/shard_map/ppermute | solution.py:71
  445.8 9.9 %fusion.18 = bf16[2,128,2048]{2,1,0:T(8,128)(2,1)} fusion(bf16[512,2,2,128]{0,3,2,1:T(8,128)(2,1)S(1)} %bitcast.252, f32[2,2,512,2048]{2,3,1,0:T(8,128)} %get-tuple-element.115, f32[2,2,512]{2,1,0:T(2,128)S(1)} %get-tuple-element.114), kind=kOutput, calls=%fused_computation.39 | convolution fusion | flops 1082654720 | bytes 18358272 | tf_op jit(solution)/shard_map/kgts,tkgd->skd/dot_general | solution.py:287
  455.7 10.6 %fusion.1 = (f32[2,2,512]{2,1,0:T(2,128)S(1)}, f32[2,2048,512,2]{2,1,3,0:T(8,128)}) fusion(f32[2,2,512,2048]{2,3,1,0:T(8,128)} %get-tuple-element.115, f32[2,2,512]{2,1,0:T(2,128)S(1)} %get-tuple-element.114, bf16[512,2,2,128]{0,3,2,1:T(8,128)(2,1)S(1)} %bitcast.253, bf16[2048,2,128,1]{2,1,0,3:T(2,128)(2,1)S(1)} %bitcast.228), kind=kOutput, calls=%fused_computation.4 | convolution fusion | flops 1086322688 | bytes 35143680 | tf_op jit(solution)/shard_map/tkgd,skd->kgts/dot_general | solution.py:286
  468.6 11.8 %fusion.3 = bf16[2,2,512,2048]{2,3,1,0:T(8,128)(2,1)S(1)} fusion(f32[2,2048,512,2]{2,1,3,0:T(8,128)} %get-tuple-element.121, f32[2,2,512]{2,1,0:T(2,128)S(1)} %get-tuple-element.120, f32[2,2,512,2048]{2,3,1,0:T(8,128)} %get-tuple-element.115, f32[2,2,512]{2,1,0:T(2,128)S(1)} %get-tuple-element.114), kind=kLoop, calls=%fused_computation.6 | loop fusion | flops 16777216 | bytes 41959424 | tf_op jit(solution)/shard_map/convert_element_type | solution.py:289
  598.7 10.8 %collective-permute-done.27 = bf16[128,2048]{1,0:T(8,128)(2,1)} collective-permute-done((bf16[128,2048]{1,0:T(8,128)(2,1)}, bf16[128,2048]{1,0:T(8,128)(2,1)}, u32[]{:S(2)}, u32[]{:S(2)}) %collective-permute-start.27) | collective-permute-done | bytes 524320 | tf_op jit(solution)/shard_map/ppermute | solution.py:71
  620.6 10.6 %collective-permute-done.15 = bf16[128,2048]{1,0:T(8,128)(2,1)} collective-permute-done((bf16[128,2048]{1,0:T(8,128)(2,1)}, bf16[128,2048]{1,0:T(8,128)(2,1)}, u32[]{:S(2)}, u32[]{:S(2)}) %collective-permute-start.15) | collective-permute-done | bytes 524320 | tf_op jit(solution)/shard_map/ppermute | solution.py:71
  642.7 53.2 %psum.7 = f32[4352]{0:T(1024)S(1)} all-reduce(f32[4352]{0:T(1024)S(1)} %pad_maximum_fusion.15), channel_id=1, replica_groups=mesh['dp'=2,'ctx'=4,'tensor'=4] {'dp','ctx','tensor'}, use_global_device_ids=true, to_apply=%region_26.27 | all-reduce | flops 4352 | bytes 34816 | tf_op jit(solution)/shard_map/psum | solution.py:332
  702.3 10.7 %collective-permute-done.18 = bf16[128,2048]{1,0:T(8,128)(2,1)S(1)} collective-permute-done((bf16[128,2048]{1,0:T(8,128)(2,1)}, bf16[128,2048]{1,0:T(8,128)(2,1)S(1)}, u32[]{:S(2)}, u32[]{:S(2)}) %collective-permute-start.18) | collective-permute-done | bytes 524320 | tf_op jit(solution)/shard_map/ppermute | solution.py:71
  713.0 9.3 %collective-permute-done.17 = bf16[128,2048]{1,0:T(8,128)(2,1)S(1)} collective-permute-done((bf16[128,2048]{1,0:T(8,128)(2,1)}, bf16[128,2048]{1,0:T(8,128)(2,1)S(1)}, u32[]{:S(2)}, u32[]{:S(2)}) %collective-permute-start.17) | collective-permute-done | bytes 524320 | tf_op jit(solution)/shard_map/ppermute | solution.py:71
  732.4 14.6 %reduce-scatter.13.cloned.1.call-done = bf16[256,1536]{1,0:T(8,128)(2,1)} async-done(((bf16[1024,1536]{1,0:T(8,128)(2,1)}), bf16[256,1536]{1,0:T(8,128)(2,1)}) %reduce-scatter.13.cloned.1.call-update) | async-done | bytes 786448 | tf_op jit(solution)/shard_map/reduce_scatter | solution.py:109
  749.5 43.4 %reduce-scatter.9.cloned.1.call-done = bf16[256,1024]{1,0:T(8,128)(2,1)} async-done(((bf16[1024,1024]{1,0:T(8,128)(2,1)}), bf16[256,1024]{1,0:T(8,128)(2,1)}) %reduce-scatter.9.cloned.1.call-update) | async-done | bytes 524304 | tf_op jit(solution)/shard_map/reduce_scatter | solution.py:109
  (411 shorter events, 318.2 us)
Async XLA Ops:
  7.2 53.6 %all-gather.7.cloned.1.call-start = ((), (), s32[]{:S(2)}) async-start(), calls=%async_computation.6 | async-start | bytes 4718592 | tf_op jit(solution)/shard_map/all_gather | solution.py:158
  9.2 233.6 %all-gather.9.cloned.1.call-start = ((), (), s32[]{:S(2)}) async-start(), calls=%async_computation.7 | async-start | bytes 2621440 | tf_op jit(solution)/shard_map/all_gather | solution.py:238
  73.2 193.9 %all-gather.11.cloned.1.call-start = ((), (), s32[]{:S(2)}) async-start(), calls=%async_computation.8 | async-start | bytes 2359296 | tf_op jit(solution)/shard_map/all_gather | solution.py:161
  73.9 232.4 %all-gather.15.cloned.1.call-start = ((), (), s32[]{:S(2)}) async-start(), calls=%async_computation.10 | async-start | bytes 7077888 | tf_op jit(solution)/shard_map/all_gather | solution.py:188
  74.5 293.5 %all-gather.13.cloned.1.call-start = ((), (), s32[]{:S(2)}) async-start(), calls=%async_computation.9 | async-start | bytes 7077888 | tf_op jit(solution)/shard_map/all_gather | solution.py:187
  107.8 38.4 %collective-permute-start.7 = (bf16[256,1536]{1,0:T(8,128)(2,1)}, bf16[256,1536]{1,0:T(8,128)(2,1)}, u32[]{:S(2)}, u32[]{:S(2)}) collective-permute-start(bf16[256,1536]{1,0:T(8,128)(2,1)} %collective-permute-done.6), channel_id=1, source_target_pairs={{0,4},{4,8},{8,12},{12,16},{16,20},{20,24},{24,28},{28,0},{1,5},{5... | collective-permute-start | bytes 2359304 | tf_op jit(solution)/shard_map/ppermute | solution.py:174
  118.1 49.8 %collective-permute-start.10 = (bf16[256,1536]{1,0:T(8,128)(2,1)}, bf16[256,1536]{1,0:T(8,128)(2,1)}, u32[]{:S(2)}, u32[]{:S(2)}) collective-permute-start(bf16[256,1536]{1,0:T(8,128)(2,1)} %param.22), channel_id=1, source_target_pairs={{4,0},{8,4},{12,8},{16,12},{20,16},{24,20},{28,24},{0,28},{5,1},{9... | collective-permute-start | bytes 2359304 | tf_op jit(solution)/shard_map/ppermute | solution.py:177
  118.1 442.4 %reduce-scatter.7.cloned.1.call-start = ((), (), s32[]{:S(2)}) async-start(), calls=%async_computation.11 | async-start | bytes 2621440 | tf_op jit(solution)/shard_map/reduce_scatter | solution.py:297
  146.2 48.6 %collective-permute-start.8 = (bf16[256,1536]{1,0:T(8,128)(2,1)}, bf16[256,1536]{1,0:T(8,128)(2,1)}, u32[]{:S(2)}, u32[]{:S(2)}) collective-permute-start(bf16[256,1536]{1,0:T(8,128)(2,1)} %collective-permute-done.7), channel_id=1, source_target_pairs={{0,4},{4,8},{8,12},{12,16},{16,20},{20,24},{24,28},{28,0},{1,5},{5... | collective-permute-start | bytes 2359304 | tf_op jit(solution)/shard_map/ppermute | solution.py:174
  167.9 47.6 %collective-permute-start.11 = (bf16[256,1536]{1,0:T(8,128)(2,1)}, bf16[256,1536]{1,0:T(8,128)(2,1)}, u32[]{:S(2)}, u32[]{:S(2)}) collective-permute-start(bf16[256,1536]{1,0:T(8,128)(2,1)} %collective-permute-done.10), channel_id=1, source_target_pairs={{4,0},{8,4},{12,8},{16,12},{20,16},{24,20},{28,24},{0,28},{5,1},{9... | collective-permute-start | bytes 2359304 | tf_op jit(solution)/shard_map/ppermute | solution.py:177
  194.8 36.6 %collective-permute-start.9 = (bf16[256,1536]{1,0:T(8,128)(2,1)}, bf16[256,1536]{1,0:T(8,128)(2,1)S(1)}, u32[]{:S(2)}, u32[]{:S(2)}) collective-permute-start(bf16[256,1536]{1,0:T(8,128)(2,1)} %collective-permute-done.8), channel_id=1, source_target_pairs={{0,4},{4,8},{8,12},{12,16},{16,20},{20,24},{24,28},{28,0},{1,5},{5... | collective-permute-start | bytes 2359304 | tf_op jit(solution)/shard_map/ppermute | solution.py:174
  215.5 63.5 %collective-permute-start.12 = (bf16[256,1536]{1,0:T(8,128)(2,1)}, bf16[256,1536]{1,0:T(8,128)(2,1)}, u32[]{:S(2)}, u32[]{:S(2)}) collective-permute-start(bf16[256,1536]{1,0:T(8,128)(2,1)} %collective-permute-done.11), channel_id=1, source_target_pairs={{4,0},{8,4},{12,8},{16,12},{20,16},{24,20},{28,24},{0,28},{5,1},{9... | collective-permute-start | bytes 2359304 | tf_op jit(solution)/shard_map/ppermute | solution.py:177
  302.3 65.7 %collective-permute-start.5 = (bf16[128,2048]{1,0:T(8,128)(2,1)S(1)}, bf16[128,2048]{1,0:T(8,128)(2,1)}, u32[]{:S(2)}, u32[]{:S(2)}) collective-permute-start(bf16[128,2048]{1,0:T(8,128)(2,1)S(1)} %multiply_convert_fusion.4), channel_id=1, source_target_pairs={{0,3},{1,2},{2,1},{3,0},{4,7},{5,6},{6,5},{7,4},{8,11},{9,10},{10,... | collective-permute-start | bytes 1572872 | tf_op jit(solution)/shard_map/ppermute | solution.py:71
  302.4 65.6 %collective-permute-start.4 = (bf16[128,2048]{1,0:T(8,128)(2,1)S(1)}, bf16[128,2048]{1,0:T(8,128)(2,1)}, u32[]{:S(2)}, u32[]{:S(2)}) collective-permute-start(bf16[128,2048]{1,0:T(8,128)(2,1)S(1)} %multiply_convert_fusion.4), channel_id=1, source_target_pairs={{0,2},{1,3},{2,0},{3,1},{4,6},{5,7},{6,4},{7,5},{8,10},{9,11},{10,... | collective-permute-start | bytes 1572872 | tf_op jit(solution)/shard_map/ppermute | solution.py:71
  304.9 63.1 %collective-permute-start.3 = (bf16[128,2048]{1,0:T(8,128)(2,1)S(1)}, bf16[128,2048]{1,0:T(8,128)(2,1)}, u32[]{:S(2)}, u32[]{:S(2)}) collective-permute-start(bf16[128,2048]{1,0:T(8,128)(2,1)S(1)} %multiply_convert_fusion.4), channel_id=1, source_target_pairs={{0,1},{1,0},{2,3},{3,2},{4,5},{5,4},{6,7},{7,6},{8,9},{9,8},{10,11... | collective-permute-start | bytes 1572872 | tf_op jit(solution)/shard_map/ppermute | solution.py:71
  489.4 151.2 %reduce-scatter.11.cloned.1.call-start = ((), (), s32[]{:S(2)}) async-start(), calls=%async_computation.13 | async-start | bytes 1310720 | tf_op jit(solution)/shard_map/reduce_scatter | solution.py:109
  505.6 221.4 %reduce-scatter.17.cloned.1.call-start = ((), (), s32[]{:S(2)}) async-start(), calls=%async_computation.16 | async-start | bytes 3932160 | tf_op jit(solution)/shard_map/reduce_scatter | solution.py:109
  511.9 218.0 %reduce-scatter.15.cloned.1.call-start = ((), (), s32[]{:S(2)}) async-start(), calls=%async_computation.15 | async-start | bytes 3932160 | tf_op jit(solution)/shard_map/reduce_scatter | solution.py:109
  525.3 221.7 %reduce-scatter.13.cloned.1.call-start = ((), (), s32[]{:S(2)}) async-start(), calls=%async_computation.14 | async-start | bytes 3932160 | tf_op jit(solution)/shard_map/reduce_scatter | solution.py:109
  543.2 249.7 %reduce-scatter.9.cloned.1.call-start = ((), (), s32[]{:S(2)}) async-start(), calls=%async_computation.12 | async-start | bytes 2621440 | tf_op jit(solution)/shard_map/reduce_scatter | solution.py:109
  588.4 42.8 %collective-permute-start.15 = (bf16[128,2048]{1,0:T(8,128)(2,1)}, bf16[128,2048]{1,0:T(8,128)(2,1)}, u32[]{:S(2)}, u32[]{:S(2)}) collective-permute-start(bf16[128,2048]{1,0:T(8,128)(2,1)} %get-tuple-element.78), channel_id=1, source_target_pairs={{0,3},{1,2},{2,1},{3,0},{4,7},{5,6},{6,5},{7,4},{8,11},{9,10},{10,... | collective-permute-start | bytes 1572872 | tf_op jit(solution)/shard_map/ppermute | solution.py:71
  637.1 63.7 %collective-permute-start.30 = (bf16[128,2048]{1,0:T(8,128)(2,1)}, bf16[128,2048]{1,0:T(8,128)(2,1)S(1)}, u32[]{:S(2)}, u32[]{:S(2)}) collective-permute-start(bf16[128,2048]{1,0:T(8,128)(2,1)} %get-tuple-element.91), channel_id=1, source_target_pairs={{0,3},{1,2},{2,1},{3,0},{4,7},{5,6},{6,5},{7,4},{8,11},{9,10},{10,... | collective-permute-start | bytes 1572872 | tf_op jit(solution)/shard_map/ppermute | solution.py:71
  638.7 62.1 %collective-permute-start.29 = (bf16[128,2048]{1,0:T(8,128)(2,1)}, bf16[128,2048]{1,0:T(8,128)(2,1)S(1)}, u32[]{:S(2)}, u32[]{:S(2)}) collective-permute-start(bf16[128,2048]{1,0:T(8,128)(2,1)} %get-tuple-element.91), channel_id=1, source_target_pairs={{0,2},{1,3},{2,0},{3,1},{4,6},{5,7},{6,4},{7,5},{8,10},{9,11},{10,... | collective-permute-start | bytes 1572872 | tf_op jit(solution)/shard_map/ppermute | solution.py:71
  640.1 60.8 %collective-permute-start.28 = (bf16[128,2048]{1,0:T(8,128)(2,1)}, bf16[128,2048]{1,0:T(8,128)(2,1)S(1)}, u32[]{:S(2)}, u32[]{:S(2)}) collective-permute-start(bf16[128,2048]{1,0:T(8,128)(2,1)} %get-tuple-element.91), channel_id=1, source_target_pairs={{0,1},{1,0},{2,3},{3,2},{4,5},{5,4},{6,7},{7,6},{8,9},{9,8},{10,11... | collective-permute-start | bytes 1572872 | tf_op jit(solution)/shard_map/ppermute | solution.py:71
  (107 other events, 2240.4 us)
Sparse Core Ops, SparseCore 0:
  10.2 50.5 all-gather.6
  73.3 79.5 all-gather.8
  154.5 51.9 all-gather.10
  208.0 92.8 all-gather.14
  302.4 65.5 all-gather.12
  489.6 41.3 reduce-scatter.6
  533.2 26.4 reduce-scatter.10
  562.1 58.9 reduce-scatter.16
  623.3 61.0 reduce-scatter.14
  686.6 60.4 reduce-scatter.12
  749.3 43.5 reduce-scatter.8
